TPU v7x, 32 devices: a whole 2x2x4 slice. The times are simulated.
32 devices in a mesh: dp: 4 (over y, x), seq: 8 (over z, core).
Axes of the slice: x: 2, y: 2, z: 4, core: 2. Of those that a mesh axis runs over, the one named last changes fastest.
Arguments:
- hidden: float32 [4, 2048, 768], P('dp', 'seq'), may hold values from -6 to 6
- cotangent: float32 [4, 2048, 768], P('dp', 'seq'), may hold values from -6 to 6
- lengths: int32 [4], P('dp'), may hold values from 1024 to 2048, as said below
- norm_gain: float32 [2, 768], P(None, 'dp'), may hold values from 0.5 to 1.5
- gate_weight: float32 [2, 768, 1536], P(None, 'dp'), may hold values from -0.21875 to 0.21875
- mix_weight: float32 [2, 768, 1792], P(None, 'dp'), may hold values from -0.21875 to 0.21875
- step_weight: float32 [2, 768, 24], P(None, 'dp'), may hold values from -0.21875 to 0.21875
- conv_kernel: float32 [2, 4, 1792], P(None, None, 'dp'), may hold values from -0.5 to 0.5
- conv_bias: float32 [2, 1792], P(None, 'dp'), may hold values from -0.5 to 0.5
- gated_gain: float32 [2, 1536], P(None, 'dp'), may hold values from 0.5 to 1.5
- out_weight: float32 [2, 1536, 768], P(None, 'dp'), may hold values from -0.15625 to 0.15625
- skip_gain: float32 [2, 24], replicated, may hold values from 0.5 to 1.5
- log_rate: float32 [2, 24], replicated, may hold values from -4 to 1
- step_bias: float32 [2, 24], replicated, may hold values from -9 to -4
Outputs:
- result: float32 [4, 2048, 768], P('dp', 'seq')
- hidden_grad: float32 [4, 2048, 768], P('dp', 'seq')
- norm_gain_grad: float32 [2, 768], P(None, 'dp')
- gate_weight_grad: float32 [2, 768, 1536], P(None, 'dp')
- mix_weight_grad: float32 [2, 768, 1792], P(None, 'dp')
- step_weight_grad: float32 [2, 768, 24], P(None, 'dp')
- conv_kernel_grad: float32 [2, 4, 1792], P(None, None, 'dp')
- conv_bias_grad: float32 [2, 1792], P(None, 'dp')
- gated_gain_grad: float32 [2, 1536], P(None, 'dp')
- out_weight_grad: float32 [2, 1536, 768], P(None, 'dp')
- skip_gain_grad: float32 [2, 24], replicated
Inputs may be any that keep to these rules, and one draw needn't show every extreme that they name: `lengths`: positions at or past a slot's length are padding; some slot has length 2048 and some slot the least length.
All inputs are finite; a program needn't handle non-finite values.
Results may differ from a plain program's by a relative error of at most 0.0003.
Values sent between devices are 32-bit elements; how exact they have to be, the bound alone decides.
A program may use at most 192 MiB of HBM per device.

v0:
```python
import jax
import jax.numpy as jnp
from jax import lax
from jax.sharding import PartitionSpec as P

EPSILON = 1e-05
HIGHEST = lax.Precision.HIGHEST


def from_behind(value, axis, steps):
    count = lax.axis_size(axis)
    first, last = (max(0, -steps), min(count, count - steps))
    return lax.ppermute(value, axis, [(source, source + steps) for source in range(first, last)])


def matmul(left, right):
    return jnp.dot(left, right, precision=HIGHEST)


def rms_scale(values):
    return lax.rsqrt(jnp.mean(values * values, axis=-1, keepdims=True) + EPSILON)


def carry_forward(totals, state_local):

    def relay_turn(turn_index, incoming):
        return from_behind(totals[:, :, None, None] * incoming + state_local, "seq", 1)

    return lax.fori_loop(0, lax.axis_size("seq") - 1, relay_turn, jnp.zeros_like(state_local))


def carry_backward(totals, state_in_grad):

    def relay_back(turn_index, incoming):
        return from_behind(totals[:, :, None, None] * incoming + state_in_grad, "seq", -1)

    return lax.fori_loop(0, lax.axis_size("seq") - 1, relay_back, jnp.zeros_like(state_in_grad))


def layer_forward(stream, weights, skip_gain, log_rate, step_bias):
    (
        norm_gain,
        gate_weight,
        mix_weight,
        step_weight,
        conv_kernel,
        conv_bias,
        gated_gain,
        out_weight,
    ) = weights
    slots, group, width = stream.shape
    inner = gated_gain.shape[0]
    heads = skip_gain.shape[0]
    head_size = inner // heads
    taps = conv_kernel.shape[0]
    flat = stream.reshape(slots * group, width)
    inv_in = rms_scale(flat)
    normed = flat * inv_in * norm_gain
    gate_pre = matmul(normed, gate_weight)
    mixed_raw = matmul(normed, mix_weight).reshape(slots, group, -1)
    step_raw = matmul(normed, step_weight).reshape(slots, group, heads)
    channels = mixed_raw.shape[-1]
    states = (channels - inner) // 2
    edge = from_behind(mixed_raw[:, group - taps + 1 :, :], "seq", 1)
    extended = jnp.concatenate([edge, mixed_raw], axis=1)
    conv_pre = conv_bias
    for tap_index in range(taps):
        conv_pre = conv_pre + conv_kernel[tap_index] * extended[:, tap_index : tap_index + group, :]
    mixed = jax.nn.silu(conv_pre)
    heads_in = mixed[..., :inner].reshape(slots, group, heads, head_size)
    input_map = mixed[..., inner : inner + states]
    output_map = mixed[..., inner + states :]
    step_size = jax.nn.softplus(step_raw + step_bias)
    rates = jnp.exp(log_rate)
    log_decay = jnp.cumsum(-rates * step_size, axis=1)
    scaled_in = heads_in * step_size[..., None]
    position = lax.iota(jnp.int32, group)
    causal = (position[:, None] >= position[None, :])[None, :, :, None]
    gaps = log_decay[:, :, None, :] - log_decay[:, None, :, :]
    decays = jnp.where(causal, jnp.exp(jnp.where(causal, gaps, 0.0)), 0.0)
    intersection = jnp.einsum("btn,bsn->bts", output_map, input_map, precision=HIGHEST)
    mixing = intersection[..., None] * decays
    diag_out = jnp.einsum("btsh,bshp->bthp", mixing, scaled_in, precision=HIGHEST)
    end_weight = jnp.exp(log_decay[:, -1:, :] - log_decay)
    state_local = jnp.einsum(
        "bshp,bsn->bhpn", scaled_in * end_weight[..., None], input_map, precision=HIGHEST
    )
    totals = jnp.exp(log_decay[:, -1, :])
    state_in = carry_forward(totals, state_local)
    lift = jnp.exp(log_decay)
    off_out = lift[..., None] * jnp.einsum(
        "btn,bhpn->bthp", output_map, state_in, precision=HIGHEST
    )
    mixed_out = diag_out + off_out + skip_gain[:, None] * heads_in
    out_flat = mixed_out.reshape(slots * group, inner)
    gate_sig = jax.nn.sigmoid(gate_pre)
    gated = out_flat * (gate_pre * gate_sig)
    inv_out = rms_scale(gated)
    normed_out = gated * inv_out * gated_gain
    branch = matmul(normed_out, out_weight)
    saved = {
        "flat": flat,
        "inv_in": inv_in,
        "normed": normed,
        "gate_pre": gate_pre,
        "gate_sig": gate_sig,
        "step_raw": step_raw,
        "extended": extended,
        "conv_pre": conv_pre,
        "heads_in": heads_in,
        "input_map": input_map,
        "output_map": output_map,
        "step_size": step_size,
        "scaled_in": scaled_in,
        "decays": decays,
        "mixing": mixing,
        "end_weight": end_weight,
        "totals": totals,
        "state_in": state_in,
        "lift": lift,
        "off_out": off_out,
        "out_flat": out_flat,
        "gated": gated,
        "inv_out": inv_out,
        "normed_out": normed_out,
    }
    return (stream + branch.reshape(slots, group, width), saved)


def layer_backward(grad, saved, weights, skip_gain, log_rate, step_bias):
    (
        norm_gain,
        gate_weight,
        mix_weight,
        step_weight,
        conv_kernel,
        conv_bias,
        gated_gain,
        out_weight,
    ) = weights
    slots, group, width = grad.shape
    inner = gated_gain.shape[0]
    heads = skip_gain.shape[0]
    head_size = inner // heads
    taps = conv_kernel.shape[0]
    flat = saved["flat"]
    inv_in = saved["inv_in"]
    normed = saved["normed"]
    gate_pre = saved["gate_pre"]
    gate_sig = saved["gate_sig"]
    heads_in = saved["heads_in"]
    input_map = saved["input_map"]
    output_map = saved["output_map"]
    scaled_in = saved["scaled_in"]
    end_weight = saved["end_weight"]
    totals = saved["totals"]
    state_in = saved["state_in"]
    mixing = saved["mixing"]
    gated = saved["gated"]
    inv_out = saved["inv_out"]
    conv_pre = saved["conv_pre"]
    extended = saved["extended"]
    channels = extended.shape[-1]
    grad_flat = grad.reshape(slots * group, width)
    out_weight_grad = matmul(saved["normed_out"].T, grad_flat)
    normed_out_grad = matmul(grad_flat, out_weight.T)
    gated_gain_grad = jnp.sum(normed_out_grad * gated * inv_out, axis=0)
    scaled = normed_out_grad * gated_gain
    gated_grad = inv_out * scaled - gated * (inv_out * inv_out * inv_out) * jnp.mean(
        scaled * gated, axis=-1, keepdims=True
    )
    gate_grad = gated_grad * saved["out_flat"] * gate_sig * (1.0 + gate_pre * (1.0 - gate_sig))
    out_grad = (gated_grad * (gate_pre * gate_sig)).reshape(slots, group, heads, head_size)
    skip_grad = jnp.sum(out_grad * heads_in, axis=(0, 1, 3))
    heads_grad = skip_gain[:, None] * out_grad
    lifted_grad = out_grad * saved["lift"][..., None]
    state_in_grad = jnp.einsum("bthp,btn->bhpn", lifted_grad, output_map, precision=HIGHEST)
    output_map_grad = jnp.einsum("bthp,bhpn->btn", lifted_grad, state_in, precision=HIGHEST)
    decay_grad = jnp.sum(out_grad * saved["off_out"], axis=-1)
    pairing = jnp.einsum("bthp,bshp->btsh", out_grad, scaled_in, precision=HIGHEST)
    scaled_grad = jnp.einsum("btsh,bthp->bshp", mixing, out_grad, precision=HIGHEST)
    intersection_grad = jnp.sum(saved["decays"] * pairing, axis=-1)
    output_map_grad = output_map_grad + jnp.einsum(
        "bts,bsn->btn", intersection_grad, input_map, precision=HIGHEST
    )
    input_map_grad = jnp.einsum("bts,btn->bsn", intersection_grad, output_map, precision=HIGHEST)
    weighted = mixing * pairing
    decay_grad = decay_grad + jnp.sum(weighted, axis=2) - jnp.sum(weighted, axis=1)
    state_out_grad = carry_backward(totals, state_in_grad)
    end_grad = jnp.sum(state_out_grad * state_in, axis=(2, 3)) * totals
    reach = jnp.einsum("bhpn,bsn->bshp", state_out_grad, input_map, precision=HIGHEST)
    scaled_grad = scaled_grad + reach * end_weight[..., None]
    input_map_grad = input_map_grad + jnp.einsum(
        "bshp,bhpn->bsn", scaled_in * end_weight[..., None], state_out_grad, precision=HIGHEST
    )
    weight_pull = jnp.sum(reach * scaled_in, axis=-1) * end_weight
    end_grad = end_grad + jnp.sum(weight_pull, axis=1)
    decay_grad = decay_grad - weight_pull
    decay_grad = jnp.concatenate(
        [decay_grad[:, :-1, :], decay_grad[:, -1:, :] + end_grad[:, None, :]], axis=1
    )
    rate_grad = jnp.flip(jnp.cumsum(jnp.flip(decay_grad, axis=1), axis=1), axis=1)
    step_grad = -jnp.exp(log_rate) * rate_grad + jnp.sum(scaled_grad * heads_in, axis=-1)
    heads_grad = heads_grad + scaled_grad * saved["step_size"][..., None]
    step_raw_grad = step_grad * jax.nn.sigmoid(saved["step_raw"] + step_bias)
    mixed_grad = jnp.concatenate(
        [heads_grad.reshape(slots, group, inner), input_map_grad, output_map_grad], axis=-1
    )
    conv_sig = jax.nn.sigmoid(conv_pre)
    pre_grad = mixed_grad * conv_sig * (1.0 + conv_pre * (1.0 - conv_sig))
    conv_bias_grad = jnp.sum(pre_grad, axis=(0, 1))
    conv_kernel_grad = jnp.stack(
        [
            jnp.sum(pre_grad * extended[:, tap_index : tap_index + group, :], axis=(0, 1))
            for tap_index in range(taps)
        ]
    )
    border = jnp.zeros((slots, taps - 1, channels), jnp.float32)
    padded_grad = jnp.concatenate([border, pre_grad, border], axis=1)
    extended_grad = conv_kernel[0] * padded_grad[:, taps - 1 : taps - 1 + group + taps - 1, :]
    for tap_index in range(1, taps):
        offset = taps - 1 - tap_index
        extended_grad = (
            extended_grad
            + conv_kernel[tap_index] * padded_grad[:, offset : offset + group + taps - 1, :]
        )
    edge_back = from_behind(extended_grad[:, : taps - 1, :], "seq", -1)
    raw_grad = extended_grad[:, taps - 1 :, :]
    raw_grad = jnp.concatenate(
        [raw_grad[:, : group - taps + 1, :], raw_grad[:, group - taps + 1 :, :] + edge_back], axis=1
    )
    raw_flat = raw_grad.reshape(slots * group, channels)
    step_flat = step_raw_grad.reshape(slots * group, heads)
    gate_weight_grad = matmul(normed.T, gate_grad)
    mix_weight_grad = matmul(normed.T, raw_flat)
    step_weight_grad = matmul(normed.T, step_flat)
    normed_grad = (
        matmul(gate_grad, gate_weight.T)
        + matmul(raw_flat, mix_weight.T)
        + matmul(step_flat, step_weight.T)
    )
    norm_gain_grad = jnp.sum(normed_grad * flat * inv_in, axis=0)
    scaled_norm = normed_grad * norm_gain
    stream_grad = (
        grad_flat
        + inv_in * scaled_norm
        - flat * (inv_in * inv_in * inv_in) * jnp.mean(scaled_norm * flat, axis=-1, keepdims=True)
    )
    weight_grads = (
        norm_gain_grad,
        gate_weight_grad,
        mix_weight_grad,
        step_weight_grad,
        conv_kernel_grad,
        conv_bias_grad,
        gated_gain_grad,
        out_weight_grad,
    )
    return (stream_grad.reshape(slots, group, width), weight_grads, skip_grad)


def on_device(
    hidden,
    cotangent,
    lengths,
    norm_gain,
    gate_weight,
    mix_weight,
    step_weight,
    conv_kernel,
    conv_bias,
    gated_gain,
    out_weight,
    skip_gain,
    log_rate,
    step_bias,
):
    slots, group, width = hidden.shape
    layers = norm_gain.shape[0]
    position = lax.axis_index("seq") * group + lax.iota(jnp.int32, group)
    mask = (position[None, :] < lengths[:, None]).astype(jnp.float32)[:, :, None]
    stream = hidden
    saved_all = []
    for layer_index in range(layers):
        weights = (
            lax.all_gather(norm_gain[layer_index], "dp", axis=0, tiled=True),
            lax.all_gather(gate_weight[layer_index], "dp", axis=0, tiled=True),
            lax.all_gather(mix_weight[layer_index], "dp", axis=0, tiled=True),
            lax.all_gather(step_weight[layer_index], "dp", axis=0, tiled=True),
            lax.all_gather(conv_kernel[layer_index], "dp", axis=1, tiled=True),
            lax.all_gather(conv_bias[layer_index], "dp", axis=0, tiled=True),
            lax.all_gather(gated_gain[layer_index], "dp", axis=0, tiled=True),
            lax.all_gather(out_weight[layer_index], "dp", axis=0, tiled=True),
        )
        stream, saved = layer_forward(
            stream, weights, skip_gain[layer_index], log_rate[layer_index], step_bias[layer_index]
        )
        saved_all.append(saved)
    result = stream * mask
    grad = cotangent * mask
    reduced_all = []
    skip_all = []
    for layer_index in reversed(range(layers)):
        weights = (
            lax.all_gather(norm_gain[layer_index], "dp", axis=0, tiled=True),
            lax.all_gather(gate_weight[layer_index], "dp", axis=0, tiled=True),
            lax.all_gather(mix_weight[layer_index], "dp", axis=0, tiled=True),
            lax.all_gather(step_weight[layer_index], "dp", axis=0, tiled=True),
            lax.all_gather(conv_kernel[layer_index], "dp", axis=1, tiled=True),
            lax.all_gather(conv_bias[layer_index], "dp", axis=0, tiled=True),
            lax.all_gather(gated_gain[layer_index], "dp", axis=0, tiled=True),
            lax.all_gather(out_weight[layer_index], "dp", axis=0, tiled=True),
        )
        grad, weight_grads, skip_grad = layer_backward(
            grad,
            saved_all[layer_index],
            weights,
            skip_gain[layer_index],
            log_rate[layer_index],
            step_bias[layer_index],
        )
        reduced = (
            lax.psum_scatter(weight_grads[0], "dp", scatter_dimension=0, tiled=True),
            lax.psum_scatter(weight_grads[1], "dp", scatter_dimension=0, tiled=True),
            lax.psum_scatter(weight_grads[2], "dp", scatter_dimension=0, tiled=True),
            lax.psum_scatter(weight_grads[3], "dp", scatter_dimension=0, tiled=True),
            lax.psum_scatter(weight_grads[4], "dp", scatter_dimension=1, tiled=True),
            lax.psum_scatter(weight_grads[5], "dp", scatter_dimension=0, tiled=True),
            lax.psum_scatter(weight_grads[6], "dp", scatter_dimension=0, tiled=True),
            lax.psum_scatter(weight_grads[7], "dp", scatter_dimension=0, tiled=True),
        )
        reduced = lax.psum(
            (
                reduced[0],
                reduced[1],
                reduced[2],
                reduced[3],
                reduced[4],
                reduced[5],
                reduced[6],
                reduced[7],
            ),
            "seq",
        )
        skip_total = lax.psum(skip_grad, ("dp", "seq"))
        reduced_all.insert(0, reduced)
        skip_all.insert(0, skip_total)
    stacked = tuple((jnp.stack([entry[member] for entry in reduced_all]) for member in range(8)))
    return (result, grad) + stacked + (jnp.stack(skip_all),)


def solution(mesh):
    return jax.shard_map(
        on_device,
        mesh=mesh,
        in_specs=(
            P("dp", "seq", None),
            P("dp", "seq", None),
            P("dp"),
            P(None, "dp"),
            P(None, "dp", None),
            P(None, "dp", None),
            P(None, "dp", None),
            P(None, None, "dp"),
            P(None, "dp"),
            P(None, "dp"),
            P(None, "dp", None),
            P(),
            P(),
            P(),
        ),
        out_specs=(
            P("dp", "seq", None),
            P("dp", "seq", None),
            P(None, "dp"),
            P(None, "dp", None),
            P(None, "dp", None),
            P(None, "dp", None),
            P(None, None, "dp"),
            P(None, "dp"),
            P(None, "dp"),
            P(None, "dp", None),
            P(),
        ),
        check_vma=False,
    )
```

profile of v0, /device:TPU:0, one launch (start us, length us, event | category | flops | bytes accessed | tf_op | source)
XLA Modules:
  0.0 1350.7 jit_solution(13960874902507613550)
XLA Ops:
  17.8 14.1 %all-gather.4 = f32[1,768,24]{2,0,1:T(1,128)S(1)} all-gather(f32[1,192,24]{2,0,1:T(1,128)S(1)} %copy.514), channel_id=6, replica_groups=mesh['dp'=4,'seq'=8] {'dp'}, dimensions={1}, use_global_device_ids=true | all-gather | bytes 92160 | tf_op jit(solution)/shard_map/all_gather | solution.py:289
  36.6 16.4 %all-reduce.18 = (f32[768]{0:T(1024)S(1)}, f32[1792]{0:T(1024)}, f32[768]{0:T(1024)S(1)}, f32[1792]{0:T(1024)}) all-reduce(f32[768]{0:T(1024)S(1)} %dynamic-update-slice.1, f32[1792]{0:T(1024)S(1)} %dynamic-update-slice, f32[768]{0:T(1024)S(1)} %dynamic-update-slice.3, ...), channel_id=4, replica_groups=mesh['dp'=4,'seq'=8] {'dp'}, use_global_device_ids=true, to_apply=%add.5 | all-reduce | flops 5120 | bytes 40960 | tf_op jit(solution)/shard_map/all_gather | solution.py:286
  56.2 20.5 %all-gather.1 = f32[1,4,1792]{1,0,2:T(1,128)S(1)} all-gather(f32[1,4,448]{1,0,2:T(1,128)S(1)} %copy.513), channel_id=3, replica_groups=mesh['dp'=4,'seq'=8] {'dp'}, dimensions={2}, use_global_device_ids=true | all-gather | bytes 35840 | tf_op jit(solution)/shard_map/all_gather | solution.py:290
  76.8 37.7 %slice_reduce_fusion.7 = (f32[1792]{0:T(1024)}, f32[1792]{0:T(1024)}, f32[1792]{0:T(1024)}, f32[1792]{0:T(1024)}) fusion(f32[1,4,1792]{1,0,2:T(1,128)S(1)} %all-gather.1), kind=kLoop, calls=%fused_computation.195 | loop fusion | bytes 57344 | tf_op jit(solution)/shard_map/slice | solution.py:68
  115.3 17.0 %all-gather.9 = f32[1,4,1792]{1,0,2:T(1,128)S(1)} all-gather(f32[1,4,448]{1,0,2:T(1,128)S(1)} %copy.515), channel_id=11, replica_groups=mesh['dp'=4,'seq'=8] {'dp'}, dimensions={2}, use_global_device_ids=true | all-gather | bytes 35840 | tf_op jit(solution)/shard_map/all_gather | solution.py:290
  132.3 37.9 %slice_reduce_fusion.3 = (f32[1792]{0:T(1024)}, f32[1792]{0:T(1024)}, f32[1792]{0:T(1024)}, f32[1792]{0:T(1024)}) fusion(f32[1,4,1792]{1,0,2:T(1,128)S(1)} %all-gather.9), kind=kLoop, calls=%fused_computation.191 | loop fusion | bytes 57344 | tf_op jit(solution)/shard_map/slice | solution.py:68
  229.8 90.3 %while.40 = (s32[]{:T(128)}, f32[1,24,64,128]{3,2,1,0:T(8,128)S(1)}, f32[1,24]{1,0:T(1,128)}, f32[1,24,64,128]{3,2,1,0:T(8,128)S(1)}, s32[]{:T(128)}) while((s32[]{:T(128)}, f32[1,24,64,128]{3,2,1,0:T(8,128)S(1)}, f32[1,24]{1,0:T(1,128)}, f32[1,24,64,128]{3,2,1,0:T(8,128)S(1)}, s32[]{:T(128)}) %tuple.134), condition=%wide.region_4.5_spmd, body=%wide.region_3.4_spmd.sunk | while | flops 393218 | bytes 5505221 | solution.py:29
  235.1 12.5 collective-permute-start
  278.5 11.5 collective-permute-start
  405.7 100.9 %while.41 = (s32[]{:T(128)}, f32[1,24,64,128]{3,2,1,0:T(8,128)S(1)}, f32[1,24]{1,0:T(1,128)}, f32[1,24,64,128]{3,2,1,0:T(8,128)}, s32[]{:T(128)}) while((s32[]{:T(128)}, f32[1,24,64,128]{3,2,1,0:T(8,128)S(1)}, f32[1,24]{1,0:T(1,128)}, f32[1,24,64,128]{3,2,1,0:T(8,128)}, s32[]{:T(128)}) %tuple.137), condition=%wide.region_10.11_spmd, body=%wide.region_9.10_spmd.sunk | while | flops 393218 | bytes 5505221 | solution.py:29
  571.8 114.4 %while.42 = (s32[]{:T(128)}, f32[1,24,64,128]{3,2,1,0:T(8,128)}, f32[1,24]{1,0:T(1,128)}, f32[1,24,64,128]{3,2,1,0:T(8,128)}, s32[]{:T(128)}) while((s32[]{:T(128)}, f32[1,24,64,128]{3,2,1,0:T(8,128)}, f32[1,24]{1,0:T(1,128)}, f32[1,24,64,128]{3,2,1,0:T(8,128)}, s32[]{:T(128)}) %tuple.182), condition=%wide.region_14.15_spmd, body=%wide.region_13.14_spmd.sunk | while | flops 393218 | bytes 5505221 | solution.py:37
  575.7 12.3 collective-permute-done.2
  591.7 13.3 collective-permute-done.2
  608.6 12.6 collective-permute-done.2
  624.9 12.6 collective-permute-done.2
  641.2 12.7 collective-permute-done.2
  657.7 12.5 collective-permute-done.2
  673.9 12.3 collective-permute-done.2
  823.5 111.6 %while.43 = (s32[]{:T(128)}, f32[1,24,64,128]{3,2,1,0:T(8,128)S(1)}, f32[1,24]{1,0:T(1,128)S(1)}, f32[1,24,64,128]{3,2,1,0:T(8,128)}, s32[]{:T(128)}) while((s32[]{:T(128)}, f32[1,24,64,128]{3,2,1,0:T(8,128)S(1)}, f32[1,24]{1,0:T(1,128)S(1)}, f32[1,24,64,128]{3,2,1,0:T(8,128)}, s32[]{:T(128)}) %tuple.181), condition=%wide.region_28.29_spmd, body=%wide.region_27.28_spmd.sunk | while | flops 393218 | bytes 5505221 | solution.py:37
  827.4 12.3 collective-permute-done.3
  843.1 12.7 collective-permute-done.3
  859.3 12.2 collective-permute-done.3
  874.9 12.6 collective-permute-done.3
  891.0 12.4 collective-permute-done.3
  906.9 12.3 collective-permute-done.3
  922.5 12.6 collective-permute-done.3
  1005.1 51.9 %reduce-scatter.23.cloned.1.call-done = f32[192,1792]{1,0:T(8,128)} async-done(((f32[768,1792]{1,0:T(8,128)}), f32[192,1792]{1,0:T(8,128)}) %reduce-scatter.23.cloned.1.call-update) | async-done | bytes 1376272 | tf_op jit(solution)/shard_map/reduce_scatter | solution.py:325
  1066.8 39.6 %all-reduce.14 = (f32[1,24]{1,0:T(1,128)S(1)}, f32[1,24]{1,0:T(1,128)S(1)}) all-reduce(f32[1,24]{1,0:T(1,128)S(1)} %bitcast.663, f32[1,24]{1,0:T(1,128)S(1)} %bitcast.664), channel_id=1, replica_groups=mesh['dp'=4,'seq'=8] {'dp','seq'}, use_global_device_ids=true, to_apply=%region_91.92 | all-reduce | flops 48 | bytes 384 | tf_op jit(solution)/shard_map/psum | solution.py:345
  1122.7 17.5 %all-reduce.17 = (f32[768]{0:T(1024)S(1)}, f32[768]{0:T(1024)S(1)}, f32[1792]{0:T(1024)S(1)}, f32[1792]{0:T(1024)S(1)}, f32[1536]{0:T(1024)S(1)}, /*index=5*/f32[1536]{0:T(1024)S(1)}) all-reduce(f32[768]{0:T(1024)S(1)} %copy-done.142, f32[768]{0:T(1024)S(1)} %get-tuple-element.129, ...), channel_id=19, replica_groups=mesh['dp'=4,'seq'=8] {'dp'}, use_global_device_ids=true, to_apply=%region_44.45.clone | all-reduce | flops 8192 | bytes 65536
  1146.3 26.1 %reduce-scatter.31.cloned.1.call-done = f32[192,24]{1,0:T(8,128)} async-done(((f32[768,24]{1,0:T(8,128)}), f32[192,24]{1,0:T(8,128)}) %reduce-scatter.31.cloned.1.call-update) | async-done | bytes 18448
  1173.3 31.6 %all-reduce.15 = (f32[1,192]{1,0:T(1,128)S(1)}, f32[1,192]{1,0:T(1,128)S(1)}, f32[1,192,24]{1,2,0:T(8,128)S(1)}, f32[1,192,24]{1,2,0:T(8,128)S(1)}, f32[1,4,448]...) all-reduce(f32[1,192]{1,0:T(1,128)S(1)} %bitcast.655, ...), channel_id=1, replica_groups=mesh['dp'=4,'seq'=8] {'seq'}, use_global_device_ids=true, to_apply=%region_45.46 | all-reduce | flops 14848 | bytes 118784 | tf_op jit(solution)/shard_map/psum | solution.py:332
  1207.9 128.5 %all-reduce.21.cloned.1.call-done = (f32[1,192,1536]{2,1,0:T(8,128)}, f32[1,192,1536]{2,1,0:T(8,128)}, f32[1,192,1792]{2,1,0:T(8,128)}, f32[1,192,1792]{2,1,0:T(...) async-done(((f32[1,192,1536]{2,1,0:T(8,128)}, f32[1,192,1536]{2,1,0:T(8,128)}, f32[1,192,1792]{2,1,0:T(8,128)}, f32[1,192,1792]{2,1,0:T(8,128)}, ...) | async-done | bytes 7471120 | tf_op jit(solution)/shard_map/psum | solution.py:332
  (720 shorter events, 690.5 us)
Async XLA Ops:
  7.2 163.7 %all-gather.23.cloned.1.call-start = ((), (), s32[]{:S(2)}) async-start(), calls=%async_computation.16 | async-start | bytes 6881280 | tf_op jit(solution)/shard_map/all_gather | solution.py:288
  10.9 323.2 %all-gather.25.cloned.1.call-start = ((), (), s32[]{:S(2)}) async-start(), calls=%async_computation.17 | async-start | bytes 5898240 | tf_op jit(solution)/shard_map/all_gather | solution.py:287
  12.5 331.4 %all-gather.27.cloned.1.call-start = ((), (), s32[]{:S(2)}) async-start(), calls=%async_computation.18 | async-start | bytes 5898240 | tf_op jit(solution)/shard_map/all_gather | solution.py:293
  15.8 338.2 %all-gather.29.cloned.1.call-start = ((), (), s32[]{:S(2)}) async-start(), calls=%async_computation.19 | async-start | bytes 6881280 | tf_op jit(solution)/shard_map/all_gather | solution.py:288
  16.4 504.2 %all-gather.31.cloned.1.call-start = ((), (), s32[]{:S(2)}) async-start(), calls=%async_computation.20 | async-start | bytes 5898240 | tf_op jit(solution)/shard_map/all_gather | solution.py:287
  17.0 513.9 %all-gather.33.cloned.1.call-start = ((), (), s32[]{:S(2)}) async-start(), calls=%async_computation.21 | async-start | bytes 5898240 | tf_op jit(solution)/shard_map/all_gather | solution.py:293
  17.6 987.4 %reduce-scatter.21.cloned.1.call-start = ((), (), s32[]{:S(2)}) async-start(), calls=%async_computation.11 | async-start | bytes 5898240 | tf_op jit(solution)/shard_map/reduce_scatter | solution.py:324
  179.0 37.5 %collective-permute-start.4 = (f32[1,3,1792]{2,1,0:T(4,128)}, f32[1,3,1792]{2,1,0:T(4,128)S(1)}, u32[]{:S(2)}, u32[]{:S(2)}) collective-permute-start(f32[1,3,1792]{2,1,0:T(4,128)} %slice.331), channel_id=1, source_target_pairs={{0,1},{1,2},{2,3},{3,4},{4,5},{5,6},{6,7},{8,9},{9,10},{10,11},{11... | collective-permute-start | bytes 64520 | tf_op jit(solution)/shard_map/ppermute | solution.py:13
  235.1 14.3 %collective-permute-start = (f32[1,24,64,128]{3,2,1,0:T(8,128)S(1)}, f32[1,24,64,128]{3,2,1,0:T(8,128)S(1)}, u32[]{:S(2)}, u32[]{:S(2)}) collective-permute-start(f32[1,24,64,128]{3,2,1,0:T(8,128)S(1)} %multiply_add_fusion.10), channel_id=1, source_target_pairs={{0,1},{1,2},{2,3},{3,4},{4,5},{5,6},{6,7},{8,9},{9,10},{10,11},{11... | collective-permute-start | bytes 2359304 | tf_op jit(solution)/shard_map/while/body/eval_jaxpr/ppermute | solution.py:13
  362.6 23.0 %collective-permute-start.5 = (f32[1,3,1792]{2,1,0:T(4,128)S(1)}, f32[1,3,1792]{2,1,0:T(4,128)S(1)}, u32[]{:S(2)}, u32[]{:S(2)}) collective-permute-start(f32[1,3,1792]{2,1,0:T(4,128)S(1)} %slice.345), channel_id=1, source_target_pairs={{0,1},{1,2},{2,3},{3,4},{4,5},{5,6},{6,7},{8,9},{9,10},{10,11},{11... | collective-permute-start | bytes 64520 | tf_op jit(solution)/shard_map/ppermute | solution.py:13
  549.3 455.7 %reduce-scatter.29.cloned.1.call-start = ((), (), s32[]{:S(2)}) async-start(), calls=%async_computation.15 | async-start | bytes 5898240 | tf_op jit(solution)/shard_map/reduce_scatter | solution.py:330
  570.8 434.3 %reduce-scatter.19.cloned.1.call-start = ((), (), s32[]{:S(2)}) async-start(), calls=%async_computation.10 | async-start | bytes 5898240 | tf_op jit(solution)/shard_map/reduce_scatter | solution.py:324
  590.4 14.6 %collective-permute-start.2 = (f32[1,24,64,128]{3,2,1,0:T(8,128)}, f32[1,24,64,128]{3,2,1,0:T(8,128)}, u32[]{:S(2)}, u32[]{:S(2)}) collective-permute-start(f32[1,24,64,128]{3,2,1,0:T(8,128)} %multiply_add_fusion.12), channel_id=1, source_target_pairs={{1,0},{2,1},{3,2},{4,3},{5,4},{6,5},{7,6},{9,8},{10,9},{11,10},{12... | collective-permute-start | bytes 2359304 | tf_op jit(solution)/shard_map/while/body/eval_jaxpr/ppermute | solution.py:13
  607.3 13.9 %collective-permute-start.2 = (f32[1,24,64,128]{3,2,1,0:T(8,128)}, f32[1,24,64,128]{3,2,1,0:T(8,128)}, u32[]{:S(2)}, u32[]{:S(2)}) collective-permute-start(f32[1,24,64,128]{3,2,1,0:T(8,128)} %multiply_add_fusion.12), channel_id=1, source_target_pairs={{1,0},{2,1},{3,2},{4,3},{5,4},{6,5},{7,6},{9,8},{10,9},{11,10},{12... | collective-permute-start | bytes 2359304 | tf_op jit(solution)/shard_map/while/body/eval_jaxpr/ppermute | solution.py:13
  623.6 13.9 %collective-permute-start.2 = (f32[1,24,64,128]{3,2,1,0:T(8,128)}, f32[1,24,64,128]{3,2,1,0:T(8,128)}, u32[]{:S(2)}, u32[]{:S(2)}) collective-permute-start(f32[1,24,64,128]{3,2,1,0:T(8,128)} %multiply_add_fusion.12), channel_id=1, source_target_pairs={{1,0},{2,1},{3,2},{4,3},{5,4},{6,5},{7,6},{9,8},{10,9},{11,10},{12... | collective-permute-start | bytes 2359304 | tf_op jit(solution)/shard_map/while/body/eval_jaxpr/ppermute | solution.py:13
  639.9 14.0 %collective-permute-start.2 = (f32[1,24,64,128]{3,2,1,0:T(8,128)}, f32[1,24,64,128]{3,2,1,0:T(8,128)}, u32[]{:S(2)}, u32[]{:S(2)}) collective-permute-start(f32[1,24,64,128]{3,2,1,0:T(8,128)} %multiply_add_fusion.12), channel_id=1, source_target_pairs={{1,0},{2,1},{3,2},{4,3},{5,4},{6,5},{7,6},{9,8},{10,9},{11,10},{12... | collective-permute-start | bytes 2359304 | tf_op jit(solution)/shard_map/while/body/eval_jaxpr/ppermute | solution.py:13
  656.4 13.8 %collective-permute-start.2 = (f32[1,24,64,128]{3,2,1,0:T(8,128)}, f32[1,24,64,128]{3,2,1,0:T(8,128)}, u32[]{:S(2)}, u32[]{:S(2)}) collective-permute-start(f32[1,24,64,128]{3,2,1,0:T(8,128)} %multiply_add_fusion.12), channel_id=1, source_target_pairs={{1,0},{2,1},{3,2},{4,3},{5,4},{6,5},{7,6},{9,8},{10,9},{11,10},{12... | collective-permute-start | bytes 2359304 | tf_op jit(solution)/shard_map/while/body/eval_jaxpr/ppermute | solution.py:13
  672.6 13.6 %collective-permute-start.2 = (f32[1,24,64,128]{3,2,1,0:T(8,128)}, f32[1,24,64,128]{3,2,1,0:T(8,128)}, u32[]{:S(2)}, u32[]{:S(2)}) collective-permute-start(f32[1,24,64,128]{3,2,1,0:T(8,128)} %multiply_add_fusion.12), channel_id=1, source_target_pairs={{1,0},{2,1},{3,2},{4,3},{5,4},{6,5},{7,6},{9,8},{10,9},{11,10},{12... | collective-permute-start | bytes 2359304 | tf_op jit(solution)/shard_map/while/body/eval_jaxpr/ppermute | solution.py:13
  737.2 23.4 %collective-permute-start.6 = (f32[1,3,1792]{2,1,0:T(4,128)}, f32[1,3,1792]{2,1,0:T(4,128)}, u32[]{:S(2)}, u32[]{:S(2)}) collective-permute-start(f32[1,3,1792]{2,1,0:T(4,128)} %slice.362), channel_id=1, source_target_pairs={{1,0},{2,1},{3,2},{4,3},{5,4},{6,5},{7,6},{9,8},{10,9},{11,10},{12... | collective-permute-start | bytes 64520 | tf_op jit(solution)/shard_map/ppermute | solution.py:13
  787.3 217.7 %reduce-scatter.27.cloned.1.call-start = ((), (), s32[]{:S(2)}) async-start(), calls=%async_computation.14 | async-start | bytes 5898240 | tf_op jit(solution)/shard_map/reduce_scatter | solution.py:330
  795.0 210.1 %reduce-scatter.25.cloned.1.call-start = ((), (), s32[]{:S(2)}) async-start(), calls=%async_computation.13 | async-start | bytes 6881280 | tf_op jit(solution)/shard_map/reduce_scatter | solution.py:325
  803.7 253.3 %reduce-scatter.23.cloned.1.call-start = ((), (), s32[]{:S(2)}) async-start(), calls=%async_computation.12 | async-start | bytes 6881280 | tf_op jit(solution)/shard_map/reduce_scatter | solution.py:325
  826.1 13.6 %collective-permute-start.3 = (f32[1,24,64,128]{3,2,1,0:T(8,128)}, f32[1,24,64,128]{3,2,1,0:T(8,128)S(1)}, u32[]{:S(2)}, u32[]{:S(2)}) collective-permute-start(f32[1,24,64,128]{3,2,1,0:T(8,128)} %multiply_add_fusion.13), channel_id=1, source_target_pairs={{1,0},{2,1},{3,2},{4,3},{5,4},{6,5},{7,6},{9,8},{10,9},{11,10},{12... | collective-permute-start | bytes 2359304 | tf_op jit(solution)/shard_map/while/body/eval_jaxpr/ppermute | solution.py:13
  841.8 14.0 %collective-permute-start.3 = (f32[1,24,64,128]{3,2,1,0:T(8,128)}, f32[1,24,64,128]{3,2,1,0:T(8,128)S(1)}, u32[]{:S(2)}, u32[]{:S(2)}) collective-permute-start(f32[1,24,64,128]{3,2,1,0:T(8,128)} %multiply_add_fusion.13), channel_id=1, source_target_pairs={{1,0},{2,1},{3,2},{4,3},{5,4},{6,5},{7,6},{9,8},{10,9},{11,10},{12... | collective-permute-start | bytes 2359304 | tf_op jit(solution)/shard_map/while/body/eval_jaxpr/ppermute | solution.py:13
  873.6 13.9 %collective-permute-start.3 = (f32[1,24,64,128]{3,2,1,0:T(8,128)}, f32[1,24,64,128]{3,2,1,0:T(8,128)S(1)}, u32[]{:S(2)}, u32[]{:S(2)}) collective-permute-start(f32[1,24,64,128]{3,2,1,0:T(8,128)} %multiply_add_fusion.13), channel_id=1, source_target_pairs={{1,0},{2,1},{3,2},{4,3},{5,4},{6,5},{7,6},{9,8},{10,9},{11,10},{12... | collective-permute-start | bytes 2359304 | tf_op jit(solution)/shard_map/while/body/eval_jaxpr/ppermute | solution.py:13
  889.7 13.7 %collective-permute-start.3 = (f32[1,24,64,128]{3,2,1,0:T(8,128)}, f32[1,24,64,128]{3,2,1,0:T(8,128)S(1)}, u32[]{:S(2)}, u32[]{:S(2)}) collective-permute-start(f32[1,24,64,128]{3,2,1,0:T(8,128)} %multiply_add_fusion.13), channel_id=1, source_target_pairs={{1,0},{2,1},{3,2},{4,3},{5,4},{6,5},{7,6},{9,8},{10,9},{11,10},{12... | collective-permute-start | bytes 2359304 | tf_op jit(solution)/shard_map/while/body/eval_jaxpr/ppermute | solution.py:13
  921.3 13.9 %collective-permute-start.3 = (f32[1,24,64,128]{3,2,1,0:T(8,128)}, f32[1,24,64,128]{3,2,1,0:T(8,128)S(1)}, u32[]{:S(2)}, u32[]{:S(2)}) collective-permute-start(f32[1,24,64,128]{3,2,1,0:T(8,128)} %multiply_add_fusion.13), channel_id=1, source_target_pairs={{1,0},{2,1},{3,2},{4,3},{5,4},{6,5},{7,6},{9,8},{10,9},{11,10},{12... | collective-permute-start | bytes 2359304 | tf_op jit(solution)/shard_map/while/body/eval_jaxpr/ppermute | solution.py:13
  991.9 149.9 %reduce-scatter.37.cloned.1.call-start = ((), (), s32[]{:S(2)}) async-start(), calls=%async_computation.25 | async-start | bytes 1146880
  994.0 148.9 %reduce-scatter.35.cloned.1.call-start = ((), (), s32[]{:S(2)}) async-start(), calls=%async_computation.24 | async-start | bytes 1146880
  995.4 149.9 %reduce-scatter.33.cloned.1.call-start = ((), (), s32[]{:S(2)}) async-start(), calls=%async_computation.23 | async-start | bytes 491520
  997.7 174.7 %reduce-scatter.31.cloned.1.call-start = ((), (), s32[]{:S(2)}) async-start(), calls=%async_computation.22 | async-start | bytes 491520
  1004.9 331.5 %all-reduce.21.cloned.1.call-start = ((), (), s32[]{:S(2)}) async-start(), calls=%async_computation.26 | async-start | bytes 14942208 | tf_op jit(solution)/shard_map/psum | solution.py:332
  (187 other events, 2146.5 us)
Sparse Core Ops, SparseCore 0:
  11.0 76.4 all-gather.22
  89.3 60.2 all-gather.24
  151.5 57.4 all-gather.26
  210.7 65.1 all-gather.28
  277.6 57.0 all-gather.30
  336.4 57.0 all-gather.32
  549.4 66.9 reduce-scatter.20
  619.4 57.0 reduce-scatter.28
  787.5 66.5 reduce-scatter.18
  856.9 57.0 reduce-scatter.26
  917.1 63.6 reduce-scatter.24
  992.0 64.8 reduce-scatter.22
  1060.5 27.1 reduce-scatter.36
  1091.0 27.0 reduce-scatter.34
  1120.7 24.5 reduce-scatter.32
  1148.0 24.3 reduce-scatter.30
  1175.1 161.2 all-reduce.20
where the time goes:
time: 1360 us; the launch traced here: 1350 us
  waiting for transfers between devices  424 us (31%)
  matrix products  246 us (18%)
  local copies, waits for them, and re-layouts  189 us (14%)
  blocking collectives  181 us (13%)
  starting transfers between devices  176 us (13%)
  other arithmetic  112 us (8%)
  between operations  20.5 us (2%)
    ppermute x32, waiting for transfers between devices, from_behind(): lax.ppermute(value, axis, [(source, source + steps) for source in range(f...  214 us
    ppermute x32, starting transfers between devices, from_behind(): lax.ppermute(value, axis, [(source, source + steps) for source in range(f...  175 us
    dot_general x22, matrix products, matmul(): return jnp.dot(left, right, precision=HIGHEST)  136 us
    psum x1, waiting for transfers between devices, on_device(): lax.psum((reduced[0], reduced[1], reduced[2], reduced[3], reduced[4], red...  128 us
    slice x2, local copies, waits for them, and re-layouts, layer_forward(): conv_kernel[tap_index] * extended[:, tap_index:tap_index + group, :]  75.7 us
    reduce_scatter x2, waiting for transfers between devices, on_device(): lax.psum_scatter(weight_grads[2], 'dp', scatter_dimension=0, tiled=True)  51.9 us
    psum x1, blocking collectives, on_device(): skip_total = lax.psum(skip_grad, ('dp', 'seq'))  39.6 us
    all_gather x2, blocking collectives, on_device(): lax.all_gather(conv_kernel[layer_index], 'dp', axis=1, tiled=True)  37.6 us
  transfers between devices with their start and end apart: 49, of which 33 were waited for; matrix products, arithmetic and copies ran while one was open for 38% of the time, Pallas kernels for 0%

commit v1 on v0

--- a/solution.py
+++ b/solution.py
@@ -1,3 +1,4 @@
+import functools
 import jax
 import jax.numpy as jnp
 from jax import lax
@@ -5,6 +6,25 @@
 
 EPSILON = 1e-05
 HIGHEST = lax.Precision.HIGHEST
+
+
+def derive_sites(row_data, pos_dim):
+    inter = lax.axis_size("dp")
+    q_next = lax.axis_index("dp")
+    lower, res, parts_out = (inter, q_next, row_data.shape[pos_dim])
+    arr_out, p_next = (row_data, 1)
+    while p_next < lower:
+        made = []
+        for i in range(lower):
+            made.append((i, (i - p_next) % lower))
+        heard = lax.ppermute(arr_out, "dp", made)
+        arr_out = jnp.concatenate([arr_out, heard], axis=pos_dim)
+        p_next = 2 * p_next
+    now = jnp.roll(arr_out, res * parts_out, axis=pos_dim)
+    return now
+
+
+push_lots_all = functools.partial(derive_sites, pos_dim=1)
 
 
 def from_behind(value, axis, steps):
@@ -287,7 +307,7 @@
             lax.all_gather(gate_weight[layer_index], "dp", axis=0, tiled=True),
             lax.all_gather(mix_weight[layer_index], "dp", axis=0, tiled=True),
             lax.all_gather(step_weight[layer_index], "dp", axis=0, tiled=True),
-            lax.all_gather(conv_kernel[layer_index], "dp", axis=1, tiled=True),
+            push_lots_all(conv_kernel[layer_index]),
             lax.all_gather(conv_bias[layer_index], "dp", axis=0, tiled=True),
             lax.all_gather(gated_gain[layer_index], "dp", axis=0, tiled=True),
             lax.all_gather(out_weight[layer_index], "dp", axis=0, tiled=True),

time: 1360 us -> 1380 us (1.015)
  waiting for transfers between devices: 424 us -> 439 us
    slice x1 -> x3, local copies, waits for them, and re-layouts: 0.16 us -> 76.2 us  [the longest x2 76.1 us: layer_backward(): conv_kernel[0] * padded_grad[:, taps - 1:taps - 1 + group + taps - 1, :]]
    slice x2, local copies, waits for them, and re-layouts: 75.7 us -> 0.74 us  [layer_forward(): conv_kernel[tap_index] * extended[:, tap_index:tap_index + group, :]]
    all_gather x2, blocking collectives: 22.4 us -> 38.5 us  [on_device(): lax.all_gather(step_weight[layer_index], 'dp', axis=0, tiled=True)]
  transfers between devices with their start and end apart: 49 -> 53, of which waited for: 33 -> 34; matrix products, arithmetic and copies ran while one was open for 38% -> 37% of each run, Pallas kernels for 0% -> 0%
where the time goes in v1:
time: 1380 us; the launch traced here: 1370 us
  waiting for transfers between devices  439 us (32%)
  matrix products  247 us (18%)
  blocking collectives  193 us (14%)
  local copies, waits for them, and re-layouts  188 us (14%)
  starting transfers between devices  174 us (13%)
  other arithmetic  110 us (8%)
  between operations  20.7 us (2%)
    ppermute x32, waiting for transfers between devices, from_behind(): lax.ppermute(value, axis, [(source, source + steps) for source in range(f...  217 us
    ppermute x32, starting transfers between devices, from_behind(): lax.ppermute(value, axis, [(source, source + steps) for source in range(f...  167 us
    dot_general x22, matrix products, matmul(): return jnp.dot(left, right, precision=HIGHEST)  136 us
    psum x1, waiting for transfers between devices, on_device(): lax.psum((reduced[0], reduced[1], reduced[2], reduced[3], reduced[4], red...  128 us
    slice x2, local copies, waits for them, and re-layouts, layer_backward(): conv_kernel[0] * padded_grad[:, taps - 1:taps - 1 + group + taps - 1, :]  76.1 us
    reduce_scatter x2, waiting for transfers between devices, on_device(): lax.psum_scatter(weight_grads[2], 'dp', scatter_dimension=0, tiled=True)  52.1 us
    psum x1, blocking collectives, on_device(): skip_total = lax.psum(skip_grad, ('dp', 'seq'))  39.6 us
    all_gather x2, blocking collectives, on_device(): lax.all_gather(step_weight[layer_index], 'dp', axis=0, tiled=True)  38.5 us
  transfers between devices with their start and end apart: 53, of which 34 were waited for; matrix products, arithmetic and copies ran while one was open for 37% of the time, Pallas kernels for 0%

profile of v1, /device:TPU:0, one launch (start us, length us, event | category | flops | bytes accessed | tf_op | source)
XLA Modules:
  0.0 1371.5 jit_solution(9845379378460673194)
XLA Ops:
  24.2 26.1 %all-gather.3 = f32[1,768,24]{2,0,1:T(1,128)S(1)} all-gather(f32[1,192,24]{2,0,1:T(1,128)S(1)} %copy.601), channel_id=5, replica_groups=mesh['dp'=4,'seq'=8] {'dp'}, dimensions={1}, use_global_device_ids=true | all-gather | bytes 92160 | tf_op jit(solution)/shard_map/all_gather | solution.py:309
  55.0 18.8 %all-reduce.18 = (f32[768]{0:T(1024)S(1)}, f32[1792]{0:T(1024)}, f32[768]{0:T(1024)S(1)}, f32[1792]{0:T(1024)}) all-reduce(f32[768]{0:T(1024)S(1)} %dynamic-update-slice.1, f32[1792]{0:T(1024)S(1)} %dynamic-update-slice, f32[768]{0:T(1024)S(1)} %dynamic-update-slice.3, ...), channel_id=3, replica_groups=mesh['dp'=4,'seq'=8] {'dp'}, use_global_device_ids=true, to_apply=%add.5 | all-reduce | flops 5120 | bytes 40960 | tf_op jit(solution)/shard_map/all_gather | solution.py:306
  104.9 12.3 all-gather.10
  142.9 86.7 %while.40 = (s32[]{:T(128)}, f32[1,24,64,128]{3,2,1,0:T(8,128)S(1)}, f32[1,24]{1,0:T(1,128)S(1)}, f32[1,24,64,128]{3,2,1,0:T(8,128)S(1)}, s32[]{:T(128)}) while((s32[]{:T(128)}, f32[1,24,64,128]{3,2,1,0:T(8,128)S(1)}, f32[1,24]{1,0:T(1,128)S(1)}, f32[1,24,64,128]{3,2,1,0:T(8,128)S(1)}, s32[]{:T(128)}) %tuple.142), condition=%wide.region_4.6_spmd, body=%wide.region_3.5_spmd.sunk | while | flops 393218 | bytes 5505221 | solution.py:49
  263.9 12.3 all-gather.29.cloned.1.call-done
  318.3 100.2 %while.41 = (s32[]{:T(128)}, f32[1,24,64,128]{3,2,1,0:T(8,128)S(1)}, f32[1,24]{1,0:T(1,128)}, f32[1,24,64,128]{3,2,1,0:T(8,128)}, s32[]{:T(128)}) while((s32[]{:T(128)}, f32[1,24,64,128]{3,2,1,0:T(8,128)S(1)}, f32[1,24]{1,0:T(1,128)}, f32[1,24,64,128]{3,2,1,0:T(8,128)}, s32[]{:T(128)}) %tuple.145), condition=%wide.region_10.12_spmd, body=%wide.region_9.11_spmd.sunk | while | flops 393218 | bytes 5505221 | solution.py:49
  373.4 11.7 collective-permute-start.1
  461.0 11.7 all-gather.14
  472.7 38.3 %slice_reduce_fusion.7 = (f32[1792]{0:T(1024)}, f32[1792]{0:T(1024)}, f32[1792]{0:T(1024)}, f32[1792]{0:T(1024)}) fusion(f32[1,4,1792]{1,0,2:T(1,128)S(1)} %all-gather.14), kind=kLoop, calls=%fused_computation.195 | loop fusion | bytes 57344 | tf_op jit(solution)/shard_map/slice | solution.py:240
  532.5 118.4 %while.42 = (s32[]{:T(128)}, f32[1,24,64,128]{3,2,1,0:T(8,128)}, f32[1,24]{1,0:T(1,128)}, f32[1,24,64,128]{3,2,1,0:T(8,128)}, s32[]{:T(128)}) while((s32[]{:T(128)}, f32[1,24,64,128]{3,2,1,0:T(8,128)}, f32[1,24]{1,0:T(1,128)}, f32[1,24,64,128]{3,2,1,0:T(8,128)}, s32[]{:T(128)}) %tuple.190), condition=%wide.region_14.16_spmd, body=%wide.region_13.15_spmd.sunk | while | flops 393218 | bytes 5505221 | solution.py:57
  536.2 11.5 collective-permute-done.2
  551.4 18.8 %collective-permute-done.2 = f32[1,24,64,128]{3,2,1,0:T(8,128)} collective-permute-done((f32[1,24,64,128]{3,2,1,0:T(8,128)}, f32[1,24,64,128]{3,2,1,0:T(8,128)}, u32[]{:S(2)}, u32[]{:S(2)}) %collective-permute-start.2) | collective-permute-done | bytes 786464 | tf_op jit(solution)/shard_map/while/body/eval_jaxpr/ppermute | solution.py:33
  573.9 12.6 collective-permute-done.2
  590.7 12.3 collective-permute-done.2
  606.7 12.2 collective-permute-done.2
  622.6 12.3 collective-permute-done.2
  638.6 12.3 collective-permute-done.2
  772.8 20.0 %all-gather.15 = f32[1,4,1792]{1,0,2:T(1,128)S(1)} all-gather(f32[1,4,448]{1,0,2:T(1,128)S(1)} %copy-done.53), channel_id=17, replica_groups=mesh['dp'=4,'seq'=8] {'dp'}, dimensions={2}, use_global_device_ids=true | all-gather | bytes 35840 | tf_op jit(solution)/shard_map/all_gather | solution.py:329
  792.7 37.7 %slice_reduce_fusion.3 = (f32[1792]{0:T(1024)S(1)}, f32[1792]{0:T(1024)S(1)}, f32[1792]{0:T(1024)S(1)}, f32[1792]{0:T(1024)S(1)}) fusion(f32[1,4,1792]{1,0,2:T(1,128)S(1)} %all-gather.15), kind=kLoop, calls=%fused_computation.191 | loop fusion | bytes 57344 | tf_op jit(solution)/shard_map/slice | solution.py:240
  845.4 111.2 %while.43 = (s32[]{:T(128)}, f32[1,24,64,128]{3,2,1,0:T(8,128)S(1)}, f32[1,24]{1,0:T(1,128)S(1)}, f32[1,24,64,128]{3,2,1,0:T(8,128)}, s32[]{:T(128)}) while((s32[]{:T(128)}, f32[1,24,64,128]{3,2,1,0:T(8,128)S(1)}, f32[1,24]{1,0:T(1,128)S(1)}, f32[1,24,64,128]{3,2,1,0:T(8,128)}, s32[]{:T(128)}) %tuple.189), condition=%wide.region_28.30_spmd, body=%wide.region_27.29_spmd.sunk | while | flops 393218 | bytes 5505221 | solution.py:57
  863.1 13.9 %collective-permute-done.3 = f32[1,24,64,128]{3,2,1,0:T(8,128)S(1)} collective-permute-done((f32[1,24,64,128]{3,2,1,0:T(8,128)}, f32[1,24,64,128]{3,2,1,0:T(8,128)S(1)}, u32[]{:S(2)}, u32[]{:S(2)}) %collective-permute-start.3) | collective-permute-done | bytes 786464 | tf_op jit(solution)/shard_map/while/body/eval_jaxpr/ppermute | solution.py:33
  880.4 12.2 collective-permute-done.3
  896.0 12.7 collective-permute-done.3
  912.1 12.6 collective-permute-done.3
  928.2 12.3 collective-permute-done.3
  944.0 12.6 collective-permute-done.3
  1025.6 52.1 %reduce-scatter.23.cloned.1.call-done = f32[192,1792]{1,0:T(8,128)} async-done(((f32[768,1792]{1,0:T(8,128)}), f32[192,1792]{1,0:T(8,128)}) %reduce-scatter.23.cloned.1.call-update) | async-done | bytes 1376272 | tf_op jit(solution)/shard_map/reduce_scatter | solution.py:345
  1087.5 39.6 %all-reduce.14 = (f32[1,24]{1,0:T(1,128)S(1)}, f32[1,24]{1,0:T(1,128)S(1)}) all-reduce(f32[1,24]{1,0:T(1,128)S(1)} %bitcast.669, f32[1,24]{1,0:T(1,128)S(1)} %bitcast.670), channel_id=1, replica_groups=mesh['dp'=4,'seq'=8] {'dp','seq'}, use_global_device_ids=true, to_apply=%region_91.93 | all-reduce | flops 48 | bytes 384 | tf_op jit(solution)/shard_map/psum | solution.py:365
  1143.4 17.5 %all-reduce.17 = (f32[768]{0:T(1024)S(1)}, f32[768]{0:T(1024)S(1)}, f32[1792]{0:T(1024)S(1)}, f32[1792]{0:T(1024)S(1)}, f32[1536]{0:T(1024)S(1)}, /*index=5*/f32[1536]{0:T(1024)S(1)}) all-reduce(f32[768]{0:T(1024)S(1)} %copy-done.140, f32[768]{0:T(1024)S(1)} %get-tuple-element.130, ...), channel_id=19, replica_groups=mesh['dp'=4,'seq'=8] {'dp'}, use_global_device_ids=true, to_apply=%region_44.46.clone | all-reduce | flops 8192 | bytes 65536
  1167.0 26.1 %reduce-scatter.31.cloned.1.call-done = f32[192,24]{1,0:T(8,128)} async-done(((f32[768,24]{1,0:T(8,128)}), f32[192,24]{1,0:T(8,128)}) %reduce-scatter.31.cloned.1.call-update) | async-done | bytes 18448
  1194.0 31.6 %all-reduce.15 = (f32[1,192]{1,0:T(1,128)S(1)}, f32[1,192]{1,0:T(1,128)S(1)}, f32[1,192,24]{1,2,0:T(8,128)S(1)}, f32[1,192,24]{1,2,0:T(8,128)S(1)}, f32[1,4,448]...) all-reduce(f32[1,192]{1,0:T(1,128)S(1)} %bitcast.661, ...), channel_id=1, replica_groups=mesh['dp'=4,'seq'=8] {'seq'}, use_global_device_ids=true, to_apply=%region_45.47 | all-reduce | flops 14848 | bytes 118784 | tf_op jit(solution)/shard_map/psum | solution.py:352
  1228.6 128.5 %all-reduce.21.cloned.1.call-done = (f32[1,192,1536]{2,1,0:T(8,128)}, f32[1,192,1536]{2,1,0:T(8,128)}, f32[1,192,1792]{2,1,0:T(8,128)}, f32[1,192,1792]{2,1,0:T(...) async-done(((f32[1,192,1536]{2,1,0:T(8,128)}, f32[1,192,1536]{2,1,0:T(8,128)}, f32[1,192,1792]{2,1,0:T(8,128)}, f32[1,192,1792]{2,1,0:T(8,128)}, ...) | async-done | bytes 7471120 | tf_op jit(solution)/shard_map/psum | solution.py:352
  (739 shorter events, 697.4 us)
Async XLA Ops:
  7.2 111.2 %all-gather.23.cloned.1.call-start = ((), (), s32[]{:S(2)}) async-start(), calls=%async_computation.16 | async-start | bytes 6881280 | tf_op jit(solution)/shard_map/all_gather | solution.py:308
  10.7 232.9 %all-gather.25.cloned.1.call-start = ((), (), s32[]{:S(2)}) async-start(), calls=%async_computation.17 | async-start | bytes 5898240 | tf_op jit(solution)/shard_map/all_gather | solution.py:307
  14.0 240.4 %all-gather.27.cloned.1.call-start = ((), (), s32[]{:S(2)}) async-start(), calls=%async_computation.18 | async-start | bytes 5898240 | tf_op jit(solution)/shard_map/all_gather | solution.py:313
  17.2 259.0 %all-gather.29.cloned.1.call-start = ((), (), s32[]{:S(2)}) async-start(), calls=%async_computation.19 | async-start | bytes 6881280 | tf_op jit(solution)/shard_map/all_gather | solution.py:308
  17.8 414.6 %all-gather.31.cloned.1.call-start = ((), (), s32[]{:S(2)}) async-start(), calls=%async_computation.20 | async-start | bytes 5898240 | tf_op jit(solution)/shard_map/all_gather | solution.py:307
  18.5 424.1 %all-gather.33.cloned.1.call-start = ((), (), s32[]{:S(2)}) async-start(), calls=%async_computation.21 | async-start | bytes 5898240 | tf_op jit(solution)/shard_map/all_gather | solution.py:313
  18.7 79.6 %collective-permute-start.7 = (f32[4,448]{0,1:T(8,128)S(1)}, f32[4,448]{0,1:T(8,128)}, u32[]{:S(2)}, u32[]{:S(2)}) collective-permute-start(f32[4,448]{0,1:T(8,128)S(1)} %bitcast.629), channel_id=1, source_target_pairs={{0,24},{8,0},{16,8},{24,16},{1,25},{9,1},{17,9},{25,17},{2,26},{10... | collective-permute-start | bytes 21512 | tf_op jit(solution)/shard_map/ppermute | solution.py:20
  22.8 77.3 %collective-permute-start.4 = (f32[4,448]{0,1:T(8,128)S(1)}, f32[4,448]{0,1:T(8,128)}, u32[]{:S(2)}, u32[]{:S(2)}) collective-permute-start(f32[4,448]{0,1:T(8,128)S(1)} %bitcast.627), channel_id=1, source_target_pairs={{0,24},{8,0},{16,8},{24,16},{1,25},{9,1},{17,9},{25,17},{2,26},{10... | collective-permute-start | bytes 21512 | tf_op jit(solution)/shard_map/ppermute | solution.py:20
  23.4 1002.1 %reduce-scatter.21.cloned.1.call-start = ((), (), s32[]{:S(2)}) async-start(), calls=%async_computation.11 | async-start | bytes 5898240 | tf_op jit(solution)/shard_map/reduce_scatter | solution.py:344
  99.4 17.8 %collective-permute-start.8 = (f32[4,896]{1,0:T(4,128)S(1)}, f32[4,896]{1,0:T(4,128)S(1)}, u32[]{:S(2)}, u32[]{:S(2)}) collective-permute-start(f32[4,896]{1,0:T(4,128)S(1)} %pad_maximum_fusion.16), channel_id=1, source_target_pairs={{0,16},{8,24},{16,0},{24,8},{1,17},{9,25},{17,1},{25,9},{2,18},{10... | collective-permute-start | bytes 43016 | tf_op jit(solution)/shard_map/ppermute | solution.py:20
  101.2 16.8 %collective-permute-start.5 = (f32[4,896]{1,0:T(4,128)S(1)}, f32[4,896]{1,0:T(4,128)S(1)}, u32[]{:S(2)}, u32[]{:S(2)}) collective-permute-start(f32[4,896]{1,0:T(4,128)S(1)} %pad_maximum_fusion.15), channel_id=1, source_target_pairs={{0,16},{8,24},{16,0},{24,8},{1,17},{9,25},{17,1},{25,9},{2,18},{10... | collective-permute-start | bytes 43016 | tf_op jit(solution)/shard_map/ppermute | solution.py:20
  373.4 13.7 %collective-permute-start.1 = (f32[1,24,64,128]{3,2,1,0:T(8,128)}, f32[1,24,64,128]{3,2,1,0:T(8,128)S(1)}, u32[]{:S(2)}, u32[]{:S(2)}) collective-permute-start(f32[1,24,64,128]{3,2,1,0:T(8,128)} %multiply_add_fusion.11), channel_id=1, source_target_pairs={{0,1},{1,2},{2,3},{3,4},{4,5},{5,6},{6,7},{8,9},{9,10},{10,11},{11... | collective-permute-start | bytes 2359304 | tf_op jit(solution)/shard_map/while/body/eval_jaxpr/ppermute | solution.py:33
  461.0 564.6 %reduce-scatter.29.cloned.1.call-start = ((), (), s32[]{:S(2)}) async-start(), calls=%async_computation.15 | async-start | bytes 5898240 | tf_op jit(solution)/shard_map/reduce_scatter | solution.py:350
  531.5 494.1 %reduce-scatter.19.cloned.1.call-start = ((), (), s32[]{:S(2)}) async-start(), calls=%async_computation.10 | async-start | bytes 5898240 | tf_op jit(solution)/shard_map/reduce_scatter | solution.py:344
  550.2 20.1 %collective-permute-start.2 = (f32[1,24,64,128]{3,2,1,0:T(8,128)}, f32[1,24,64,128]{3,2,1,0:T(8,128)}, u32[]{:S(2)}, u32[]{:S(2)}) collective-permute-start(f32[1,24,64,128]{3,2,1,0:T(8,128)} %multiply_add_fusion.12), channel_id=1, source_target_pairs={{1,0},{2,1},{3,2},{4,3},{5,4},{6,5},{7,6},{9,8},{10,9},{11,10},{12... | collective-permute-start | bytes 2359304 | tf_op jit(solution)/shard_map/while/body/eval_jaxpr/ppermute | solution.py:33
  572.7 13.9 %collective-permute-start.2 = (f32[1,24,64,128]{3,2,1,0:T(8,128)}, f32[1,24,64,128]{3,2,1,0:T(8,128)}, u32[]{:S(2)}, u32[]{:S(2)}) collective-permute-start(f32[1,24,64,128]{3,2,1,0:T(8,128)} %multiply_add_fusion.12), channel_id=1, source_target_pairs={{1,0},{2,1},{3,2},{4,3},{5,4},{6,5},{7,6},{9,8},{10,9},{11,10},{12... | collective-permute-start | bytes 2359304 | tf_op jit(solution)/shard_map/while/body/eval_jaxpr/ppermute | solution.py:33
  621.3 13.6 collective-permute-start.2
  637.3 13.6 collective-permute-start.2
  701.2 23.4 %collective-permute-start.10 = (f32[1,3,1792]{2,1,0:T(4,128)}, f32[1,3,1792]{2,1,0:T(4,128)}, u32[]{:S(2)}, u32[]{:S(2)}) collective-permute-start(f32[1,3,1792]{2,1,0:T(4,128)} %slice.390), channel_id=1, source_target_pairs={{1,0},{2,1},{3,2},{4,3},{5,4},{6,5},{7,6},{9,8},{10,9},{11,10},{12... | collective-permute-start | bytes 64520 | tf_op jit(solution)/shard_map/ppermute | solution.py:33
  751.3 274.3 %reduce-scatter.27.cloned.1.call-start = ((), (), s32[]{:S(2)}) async-start(), calls=%async_computation.14 | async-start | bytes 5898240 | tf_op jit(solution)/shard_map/reduce_scatter | solution.py:350
  759.0 266.7 %reduce-scatter.25.cloned.1.call-start = ((), (), s32[]{:S(2)}) async-start(), calls=%async_computation.13 | async-start | bytes 6881280 | tf_op jit(solution)/shard_map/reduce_scatter | solution.py:345
  767.7 310.0 %reduce-scatter.23.cloned.1.call-start = ((), (), s32[]{:S(2)}) async-start(), calls=%async_computation.12 | async-start | bytes 6881280 | tf_op jit(solution)/shard_map/reduce_scatter | solution.py:345
  861.8 15.2 %collective-permute-start.3 = (f32[1,24,64,128]{3,2,1,0:T(8,128)}, f32[1,24,64,128]{3,2,1,0:T(8,128)S(1)}, u32[]{:S(2)}, u32[]{:S(2)}) collective-permute-start(f32[1,24,64,128]{3,2,1,0:T(8,128)} %multiply_add_fusion.13), channel_id=1, source_target_pairs={{1,0},{2,1},{3,2},{4,3},{5,4},{6,5},{7,6},{9,8},{10,9},{11,10},{12... | collective-permute-start | bytes 2359304 | tf_op jit(solution)/shard_map/while/body/eval_jaxpr/ppermute | solution.py:33
  894.7 13.9 %collective-permute-start.3 = (f32[1,24,64,128]{3,2,1,0:T(8,128)}, f32[1,24,64,128]{3,2,1,0:T(8,128)S(1)}, u32[]{:S(2)}, u32[]{:S(2)}) collective-permute-start(f32[1,24,64,128]{3,2,1,0:T(8,128)} %multiply_add_fusion.13), channel_id=1, source_target_pairs={{1,0},{2,1},{3,2},{4,3},{5,4},{6,5},{7,6},{9,8},{10,9},{11,10},{12... | collective-permute-start | bytes 2359304 | tf_op jit(solution)/shard_map/while/body/eval_jaxpr/ppermute | solution.py:33
  910.8 13.9 %collective-permute-start.3 = (f32[1,24,64,128]{3,2,1,0:T(8,128)}, f32[1,24,64,128]{3,2,1,0:T(8,128)S(1)}, u32[]{:S(2)}, u32[]{:S(2)}) collective-permute-start(f32[1,24,64,128]{3,2,1,0:T(8,128)} %multiply_add_fusion.13), channel_id=1, source_target_pairs={{1,0},{2,1},{3,2},{4,3},{5,4},{6,5},{7,6},{9,8},{10,9},{11,10},{12... | collective-permute-start | bytes 2359304 | tf_op jit(solution)/shard_map/while/body/eval_jaxpr/ppermute | solution.py:33
  926.9 13.6 collective-permute-start.3
  942.7 13.9 %collective-permute-start.3 = (f32[1,24,64,128]{3,2,1,0:T(8,128)}, f32[1,24,64,128]{3,2,1,0:T(8,128)S(1)}, u32[]{:S(2)}, u32[]{:S(2)}) collective-permute-start(f32[1,24,64,128]{3,2,1,0:T(8,128)} %multiply_add_fusion.13), channel_id=1, source_target_pairs={{1,0},{2,1},{3,2},{4,3},{5,4},{6,5},{7,6},{9,8},{10,9},{11,10},{12... | collective-permute-start | bytes 2359304 | tf_op jit(solution)/shard_map/while/body/eval_jaxpr/ppermute | solution.py:33
  1012.4 150.1 %reduce-scatter.37.cloned.1.call-start = ((), (), s32[]{:S(2)}) async-start(), calls=%async_computation.25 | async-start | bytes 1146880
  1014.5 149.1 %reduce-scatter.35.cloned.1.call-start = ((), (), s32[]{:S(2)}) async-start(), calls=%async_computation.24 | async-start | bytes 1146880
  1015.9 150.1 %reduce-scatter.33.cloned.1.call-start = ((), (), s32[]{:S(2)}) async-start(), calls=%async_computation.23 | async-start | bytes 491520
  1018.2 174.8 %reduce-scatter.31.cloned.1.call-start = ((), (), s32[]{:S(2)}) async-start(), calls=%async_computation.22 | async-start | bytes 491520
  1025.4 331.7 %all-reduce.21.cloned.1.call-start = ((), (), s32[]{:S(2)}) async-start(), calls=%async_computation.26 | async-start | bytes 14942208 | tf_op jit(solution)/shard_map/psum | solution.py:352
  (191 other events, 2115.7 us)
Sparse Core Ops, SparseCore 0:
  10.8 79.9 all-gather.22
  92.7 59.2 all-gather.24
  153.8 57.0 all-gather.26
  212.6 63.6 all-gather.28
  277.9 57.0 all-gather.30
  336.7 57.0 all-gather.32
  461.1 69.9 reduce-scatter.20
  534.0 69.7 reduce-scatter.28
  751.4 74.4 reduce-scatter.18
  828.7 57.0 reduce-scatter.26
  888.9 63.6 reduce-scatter.24
  1012.5 65.1 reduce-scatter.22
  1081.2 27.1 reduce-scatter.36
  1111.8 27.0 reduce-scatter.34
  1141.5 24.5 reduce-scatter.32
  1168.7 24.3 reduce-scatter.30
  1195.8 161.2 all-reduce.20
